TPU v7x, 32 devices: a whole 2x2x4 slice. The times are simulated.
32 devices in a mesh: row: 4 (over x, core), col: 8 (over z, y).
Axes of the slice: x: 2, y: 2, z: 4, core: 2. Of those that a mesh axis runs over, the one named last changes fastest.
Arguments:
- embeddings: bfloat16 [4096, 512], P(('row', 'col')), may hold values from -6 to 6
- sketch: bfloat16 [4096, 64], P(('row', 'col')), may hold values from -240 to 240
Outputs:
- basis: float32 [4096, 64], P(('row', 'col'))
- first_pass: float32 [4096, 64], P(('row', 'col'))
All inputs are finite; a program needn't handle non-finite values.
Results may differ from a plain program's by a relative error of at most 0.00205.
Values may be sent and summed in bfloat16 or wider, within the bound.
No kernel may reach another device: no remote copies, remote signals or barrier semaphores. Data moves between devices by JAX's collectives and lax.ppermute only.
A program may use at most 64 MiB of HBM per device.

v0:
```python
import jax
import jax.numpy as jnp
from jax import lax
from jax.sharding import PartitionSpec as P


def squares_of(points):
    return jnp.sum(jnp.square(points.astype(jnp.float32)), axis=1)


def kernel_tile(left, right, left_sq, right_sq, gamma):
    cross = lax.dot_general(
        left, right, (((1,), (1,)), ((), ())), preferred_element_type=jnp.float32
    )
    dist = left_sq[:, None] + right_sq[None, :] - 2.0 * cross
    return jnp.exp(-gamma * dist).astype(jnp.bfloat16)


def product_of(left, right):
    return lax.dot_general(
        left,
        right,
        (((0,), (0,)), ((), ())),
        precision=lax.Precision.HIGHEST,
        preferred_element_type=jnp.float32,
    )


def per_device(embeddings, sketch):
    width = embeddings.shape[1]
    gamma = 3.0 / width
    own_points = lax.all_gather(embeddings, "row", axis=0, tiled=True)
    own_sq = squares_of(own_points)
    empty = jnp.zeros((own_points.shape[0], sketch.shape[1]), jnp.float32)
    total = empty
    points = lax.all_gather(embeddings, "col", axis=0, tiled=True)
    tests = lax.all_gather(sketch, "col", axis=0, tiled=True)
    count = points.shape[0]
    size = 512

    def step(carry, block):
        block_points, block_tests = block
        tile = kernel_tile(own_points, block_points, own_sq, squares_of(block_points), gamma)
        return (carry + jnp.dot(tile, block_tests, preferred_element_type=jnp.float32), None)

    stacked = (
        points.reshape(count // size, size, width),
        tests.reshape(count // size, size, tests.shape[1]),
    )
    total, unused = lax.scan(step, total, stacked)
    sketched = lax.psum_scatter(total, "row", scatter_dimension=0, tiled=True)
    core = lax.psum(product_of(sketch.astype(jnp.float32), sketched), ("row", "col"))
    lower = jnp.linalg.cholesky(core)
    first = jax.scipy.linalg.solve_triangular(lower, sketched.T, lower=True).T
    gram_two = lax.psum(product_of(first, first), ("row", "col"))
    lower_two = jnp.linalg.cholesky(gram_two)
    second = jax.scipy.linalg.solve_triangular(lower_two, first.T, lower=True).T
    total_points = sketched.shape[0] * lax.axis_size("row") * lax.axis_size("col")
    scale = jnp.sqrt(jnp.float32(total_points))
    return (second * scale, first * scale)


def solution(mesh):
    placed = (P(("row", "col"), None), P(("row", "col"), None))
    return jax.shard_map(
        per_device,
        mesh=mesh,
        in_specs=placed,
        out_specs=(P(("row", "col"), None), P(("row", "col"), None)),
        check_vma=False,
    )
```

profile of v0, /device:TPU:0, one launch (start us, length us, event | category | flops | bytes accessed | tf_op | source)
XLA Modules:
  0.0 193.4 jit_solution(8559707278417701284)
XLA Ops:
  7.2 0.0 copy-start.3
  7.2 0.0 all-gather.2.cloned.1.call-start
  7.2 0.7 all-gather.2.cloned.1.call-update
  7.9 0.0 reduce-scatter.2.cloned.1.call-start
  8.0 0.0 copy-done.3
  8.0 28.2 %all_gather.11 = bf16[1024,64]{0,1:T(8,128)(2,1)S(1)} all-gather(bf16[128,64]{0,1:T(8,128)(2,1)S(1)} %copy-done.3), channel_id=1, replica_groups=mesh['row'=4,'col'=8] {'col'}, dimensions={0}, use_global_device_ids=true | all-gather | bytes 147456 | tf_op jit(solution)/shard_map/all_gather | solution.py:37
  36.2 0.0 copy-start
  36.2 0.2 copy.4
  36.4 0.7 copy-done
  37.1 7.2 %all_gather.9 = bf16[512,512]{1,0:T(8,128)(2,1)S(1)} all-gather(bf16[128,512]{1,0:T(8,128)(2,1)S(1)} %copy-done), channel_id=1, replica_groups=mesh['row'=4,'col'=8] {'row'}, dimensions={0}, use_global_device_ids=true | all-gather | bytes 655360 | tf_op jit(solution)/shard_map/all_gather | solution.py:32
  44.3 0.2 multiply_reduce_fusion.1
  44.5 9.1 %all-gather.2.cloned.1.call-done = bf16[1024,512]{1,0:T(8,128)(2,1)} async-done(((bf16[128,512]{1,0:T(8,128)(2,1)}), bf16[1024,512]{1,0:T(8,128)(2,1)}) %all-gather.2.cloned.1.call-update) | async-done | bytes 1048592 | tf_op jit(solution)/shard_map/all_gather | solution.py:36
  53.6 6.2 %while.11 = (s32[]{:T(128)}, f32[512,64]{0,1:T(8,128)S(1)}, f32[512]{0:T(512)S(1)}, bf16[2,512,512]{2,1,0:T(8,128)(2,1)}, bf16[512,512]{1,0:T(8,128)(2,1)S(1)}, ...) while((s32[]{:T(128)}, f32[512,64]{0,1:T(8,128)S(1)}, f32[512]{0:T(512)S(1)}, ...), condition=%wide.region_3.4_spmd.clone, body=%wide.region_1.3_spmd.clone.sunk | while | flops 304152064 | bytes 1973347 | solution.py:50
  53.6 1.2 multiply_reduce_fusion.3
  54.8 1.8 fusion.47
  56.6 1.2 multiply_reduce_fusion.3
  57.9 1.8 fusion.47
  59.7 0.0 copy-start.2
  59.7 0.6 copy-done.2
  60.4 0.0 reduce-scatter.2.cloned.1.call-update
  60.4 18.5 %reduce-scatter.2.cloned.1.call-done = f32[128,64]{0,1:T(8,128)} async-done(((f32[512,64]{0,1:T(8,128)}), f32[128,64]{0,1:T(8,128)}) %reduce-scatter.2.cloned.1.call-update) | async-done | bytes 32784 | tf_op jit(solution)/shard_map/reduce_scatter | solution.py:51
  78.9 0.9 convolution_bitcast_fusion
  79.8 39.4 %psum.14 = f32[64,64]{0,1:T(8,128)S(1)} all-reduce(f32[64,64]{0,1:T(8,128)S(1)} %convolution_bitcast_fusion), channel_id=1, replica_groups=mesh['row'=4,'col'=8] {'row','col'}, use_global_device_ids=true, to_apply=%region_5.6 | all-reduce | flops 4096 | bytes 32768 | tf_op jit(solution)/shard_map/psum | solution.py:52
  119.3 0.1 copy.5
  119.3 5.8 %cholesky.44 = f32[64,64]{1,0:T(8,128)S(1)} custom-call(f32[64,64]{1,0:T(8,128)S(1)} %fusion.30), custom_call_target="Cholesky" | custom-call | tf_op jit(solution)/shard_map/jit(cholesky)/cholesky | solution.py:53
  125.2 0.6 compare_reduce_fusion.1
  125.9 0.0 copy-start.1
  125.9 0.7 fusion.23
  126.5 4.9 %custom-call.7 = f32[1,64,64]{1,2,0:T(8,128)S(1)} custom-call(f32[1,64,64]{2,1,0:T(8,128)S(1)} %fusion.23), custom_call_target="InvertDiagBlocksLowerTriangular" | custom-call | tf_op jit(solution)/shard_map/jit(_solve_triangular)/triangular_solve | solution.py:54
  131.4 0.0 copy-done.1
  131.5 0.2 fusion.27
  131.7 0.2 fusion.33
  131.9 0.6 multiply_bitcast_fusion
  132.5 41.0 %psum.15 = f32[64,64]{0,1:T(8,128)S(1)} all-reduce(f32[64,64]{0,1:T(8,128)S(1)} %fusion.33), channel_id=1, replica_groups=mesh['row'=4,'col'=8] {'row','col'}, use_global_device_ids=true, to_apply=%region_8.11 | all-reduce | flops 4096 | bytes 32768 | tf_op jit(solution)/shard_map/psum | solution.py:55
  173.5 0.1 copy.7
  173.6 5.8 %cholesky.55 = f32[64,64]{1,0:T(8,128)S(1)} custom-call(f32[64,64]{1,0:T(8,128)S(1)} %fusion.26), custom_call_target="Cholesky" | custom-call | tf_op jit(solution)/shard_map/jit(cholesky)/cholesky | solution.py:56
  179.5 0.6 compare_reduce_fusion
  180.2 0.7 fusion.24
  180.8 4.9 %custom-call.8 = f32[1,64,64]{1,2,0:T(8,128)S(1)} custom-call(f32[1,64,64]{2,1,0:T(8,128)S(1)} %fusion.24), custom_call_target="InvertDiagBlocksLowerTriangular" | custom-call | tf_op jit(solution)/shard_map/jit(_solve_triangular)/triangular_solve | solution.py:57
  185.7 0.9 fusion.22
  (5 shorter events, 0.1 us)
Async XLA Ops:
  7.2 0.8 copy-start.3
  7.2 46.4 %all-gather.2.cloned.1.call-start = ((), (), s32[]{:S(2)}) async-start(), calls=%async_computation.1 | async-start | bytes 1179648 | tf_op jit(solution)/shard_map/all_gather | solution.py:36
  7.9 71.0 %reduce-scatter.2.cloned.1.call-start = ((), (), s32[]{:S(2)}) async-start(), calls=%async_computation.2 | async-start | bytes 163840 | tf_op jit(solution)/shard_map/reduce_scatter | solution.py:51
  36.2 0.9 copy-start
  59.7 0.6 copy-start.2
  125.9 5.6 %copy-start.1 = (f32[128,64]{0,1:T(8,128)S(1)}, f32[128,64]{0,1:T(8,128)}, u32[]{:S(2)}) copy-start(f32[128,64]{0,1:T(8,128)} %reduce-scatter.2.cloned.1.call-done) | copy-start | bytes 98308
Sparse Core Ops, SparseCore 0:
  10.1 43.4 all-gather.1
  60.5 18.3 reduce-scatter.1
where the time goes:
time: 194 us; the launch traced here: 193 us
  blocking collectives  116 us (60%)
  waiting for transfers between devices  28.3 us (15%)
  other arithmetic  27.4 us (14%)
  between operations  14.2 us (7%)
  matrix products  5.88 us (3%)
    psum x1, blocking collectives, per_device(): gram_two = lax.psum(product_of(first, first), ('row', 'col'))  41 us
    psum x1, blocking collectives, per_device(): lax.psum(product_of(sketch.astype(jnp.float32), sketched), ('row', 'col'))  39.4 us
    all_gather x1, blocking collectives, per_device(): tests = lax.all_gather(sketch, 'col', axis=0, tiled=True)  28.2 us
    reduce_scatter x1, waiting for transfers between devices, per_device(): sketched = lax.psum_scatter(total, 'row', scatter_dimension=0, tiled=True)  18.5 us
    all_gather x1, waiting for transfers between devices, per_device(): points = lax.all_gather(embeddings, 'col', axis=0, tiled=True)  9.11 us
    all_gather x1, blocking collectives, per_device(): own_points = lax.all_gather(embeddings, 'row', axis=0, tiled=True)  7.18 us
    another operation x3, other arithmetic, per_device(): lower_two = jnp.linalg.cholesky(gram_two)  6.52 us
    another operation x3, other arithmetic, per_device(): lower = jnp.linalg.cholesky(core)  6.52 us
  transfers between devices with their start and end apart: 2, of which 2 were waited for; matrix products, arithmetic and copies ran while one was open for 0% of the time, Pallas kernels for 0%

commit v1 on v0

--- a/solution.py
+++ b/solution.py
@@ -49,7 +49,7 @@
     )
     total, unused = lax.scan(step, total, stacked)
     sketched = lax.psum_scatter(total, "row", scatter_dimension=0, tiled=True)
-    core = lax.psum(product_of(sketch.astype(jnp.float32), sketched), ("row", "col"))
+    core = lax.psum(lax.psum(product_of(sketch.astype(jnp.float32), sketched), "row"), "col")
     lower = jnp.linalg.cholesky(core)
     first = jax.scipy.linalg.solve_triangular(lower, sketched.T, lower=True).T
     gram_two = lax.psum(product_of(first, first), ("row", "col"))

time: 194 us -> 199 us (1.026)
  blocking collectives: 116 us -> 120 us
    psum x1 -> x2, blocking collectives: 39.4 us -> 47.5 us  [the longest x1 37.2 us: per_device(): lax.psum(lax.psum(product_of(sketch.astype(jnp.float32), sketched), 'row'...]
    psum x1, blocking collectives: 41 us -> 36.9 us  [per_device(): gram_two = lax.psum(product_of(first, first), ('row', 'col'))]
where the time goes in v1:
time: 199 us; the launch traced here: 197 us
  blocking collectives  120 us (60%)
  waiting for transfers between devices  28.3 us (14%)
  other arithmetic  27.4 us (14%)
  between operations  14.2 us (7%)
  matrix products  5.88 us (3%)
    psum x1, blocking collectives, per_device(): lax.psum(lax.psum(product_of(sketch.astype(jnp.float32), sketched), 'row'...  37.2 us
    psum x1, blocking collectives, per_device(): gram_two = lax.psum(product_of(first, first), ('row', 'col'))  36.9 us
    all_gather x1, blocking collectives, per_device(): tests = lax.all_gather(sketch, 'col', axis=0, tiled=True)  28.2 us
    reduce_scatter x1, waiting for transfers between devices, per_device(): sketched = lax.psum_scatter(total, 'row', scatter_dimension=0, tiled=True)  18.5 us
    psum x1, blocking collectives, per_device(): lax.psum(product_of(sketch.astype(jnp.float32), sketched), 'row')  10.3 us
    all_gather x1, waiting for transfers between devices, per_device(): points = lax.all_gather(embeddings, 'col', axis=0, tiled=True)  9.11 us
    all_gather x1, blocking collectives, per_device(): own_points = lax.all_gather(embeddings, 'row', axis=0, tiled=True)  7.18 us
    another operation x3, other arithmetic, per_device(): lower = jnp.linalg.cholesky(core)  6.52 us
  transfers between devices with their start and end apart: 2, of which 2 were waited for; matrix products, arithmetic and copies ran while one was open for 0% of the time, Pallas kernels for 0%

profile of v1, /device:TPU:0, one launch (start us, length us, event | category | flops | bytes accessed | tf_op | source)
XLA Modules:
  0.0 197.4 jit_solution(5714222830586120763)
XLA Ops:
  7.2 0.0 copy-start.3
  7.2 0.0 all-gather.2.cloned.1.call-start
  7.2 0.7 all-gather.2.cloned.1.call-update
  7.9 0.0 reduce-scatter.2.cloned.1.call-start
  8.0 0.0 copy-done.3
  8.0 28.2 %all_gather.11 = bf16[1024,64]{0,1:T(8,128)(2,1)S(1)} all-gather(bf16[128,64]{0,1:T(8,128)(2,1)S(1)} %copy-done.3), channel_id=1, replica_groups=mesh['row'=4,'col'=8] {'col'}, dimensions={0}, use_global_device_ids=true | all-gather | bytes 147456 | tf_op jit(solution)/shard_map/all_gather | solution.py:37
  36.2 0.0 copy-start
  36.2 0.2 copy.4
  36.4 0.7 copy-done
  37.1 7.2 %all_gather.9 = bf16[512,512]{1,0:T(8,128)(2,1)S(1)} all-gather(bf16[128,512]{1,0:T(8,128)(2,1)S(1)} %copy-done), channel_id=1, replica_groups=mesh['row'=4,'col'=8] {'row'}, dimensions={0}, use_global_device_ids=true | all-gather | bytes 655360 | tf_op jit(solution)/shard_map/all_gather | solution.py:32
  44.3 0.2 multiply_reduce_fusion.1
  44.5 9.1 %all-gather.2.cloned.1.call-done = bf16[1024,512]{1,0:T(8,128)(2,1)} async-done(((bf16[128,512]{1,0:T(8,128)(2,1)}), bf16[1024,512]{1,0:T(8,128)(2,1)}) %all-gather.2.cloned.1.call-update) | async-done | bytes 1048592 | tf_op jit(solution)/shard_map/all_gather | solution.py:36
  53.6 6.2 %while.11 = (s32[]{:T(128)}, f32[512,64]{0,1:T(8,128)S(1)}, f32[512]{0:T(512)S(1)}, bf16[2,512,512]{2,1,0:T(8,128)(2,1)}, bf16[512,512]{1,0:T(8,128)(2,1)S(1)}, ...) while((s32[]{:T(128)}, f32[512,64]{0,1:T(8,128)S(1)}, f32[512]{0:T(512)S(1)}, ...), condition=%wide.region_3.4_spmd.clone, body=%wide.region_1.3_spmd.clone.sunk | while | flops 304152064 | bytes 1973347 | solution.py:50
  53.6 1.2 multiply_reduce_fusion.3
  54.8 1.8 fusion.47
  56.6 1.2 multiply_reduce_fusion.3
  57.9 1.8 fusion.47
  59.7 0.0 copy-start.2
  59.7 0.6 copy-done.2
  60.4 0.0 reduce-scatter.2.cloned.1.call-update
  60.4 18.5 %reduce-scatter.2.cloned.1.call-done = f32[128,64]{0,1:T(8,128)} async-done(((f32[512,64]{0,1:T(8,128)}), f32[128,64]{0,1:T(8,128)}) %reduce-scatter.2.cloned.1.call-update) | async-done | bytes 32784 | tf_op jit(solution)/shard_map/reduce_scatter | solution.py:51
  78.9 0.9 convolution_bitcast_fusion
  79.8 10.3 %psum.21 = f32[64,64]{0,1:T(8,128)S(1)} all-reduce(f32[64,64]{0,1:T(8,128)S(1)} %convolution_bitcast_fusion), channel_id=1, replica_groups=mesh['row'=4,'col'=8] {'row'}, use_global_device_ids=true, to_apply=%region_5.6 | all-reduce | flops 4096 | bytes 32768 | tf_op jit(solution)/shard_map/psum | solution.py:52
  90.1 37.2 %psum.22 = f32[64,64]{0,1:T(8,128)S(1)} all-reduce(f32[64,64]{0,1:T(8,128)S(1)} %psum.21), channel_id=1, replica_groups=mesh['row'=4,'col'=8] {'col'}, use_global_device_ids=true, to_apply=%region_6.7 | all-reduce | flops 4096 | bytes 32768 | tf_op jit(solution)/shard_map/psum | solution.py:52
  127.3 0.1 copy.5
  127.4 5.8 %cholesky.44 = f32[64,64]{1,0:T(8,128)S(1)} custom-call(f32[64,64]{1,0:T(8,128)S(1)} %fusion.30), custom_call_target="Cholesky" | custom-call | tf_op jit(solution)/shard_map/jit(cholesky)/cholesky | solution.py:53
  133.3 0.6 compare_reduce_fusion.1
  133.9 0.0 copy-start.1
  133.9 0.7 fusion.23
  134.6 4.9 %custom-call.7 = f32[1,64,64]{1,2,0:T(8,128)S(1)} custom-call(f32[1,64,64]{2,1,0:T(8,128)S(1)} %fusion.23), custom_call_target="InvertDiagBlocksLowerTriangular" | custom-call | tf_op jit(solution)/shard_map/jit(_solve_triangular)/triangular_solve | solution.py:54
  139.5 0.0 copy-done.1
  139.5 0.2 fusion.27
  139.8 0.2 fusion.33
  140.0 0.6 multiply_bitcast_fusion
  140.6 36.9 %psum.23 = f32[64,64]{0,1:T(8,128)S(1)} all-reduce(f32[64,64]{0,1:T(8,128)S(1)} %fusion.33), channel_id=1, replica_groups=mesh['row'=4,'col'=8] {'row','col'}, use_global_device_ids=true, to_apply=%region_9.12 | all-reduce | flops 4096 | bytes 32768 | tf_op jit(solution)/shard_map/psum | solution.py:55
  177.5 0.1 copy.7
  177.6 5.8 %cholesky.55 = f32[64,64]{1,0:T(8,128)S(1)} custom-call(f32[64,64]{1,0:T(8,128)S(1)} %fusion.26), custom_call_target="Cholesky" | custom-call | tf_op jit(solution)/shard_map/jit(cholesky)/cholesky | solution.py:56
  183.5 0.6 compare_reduce_fusion
  184.1 0.7 fusion.24
  184.8 4.9 %custom-call.8 = f32[1,64,64]{1,2,0:T(8,128)S(1)} custom-call(f32[1,64,64]{2,1,0:T(8,128)S(1)} %fusion.24), custom_call_target="InvertDiagBlocksLowerTriangular" | custom-call | tf_op jit(solution)/shard_map/jit(_solve_triangular)/triangular_solve | solution.py:57
  189.7 0.9 fusion.22
  (5 shorter events, 0.1 us)
Async XLA Ops:
  7.2 0.8 copy-start.3
  7.2 46.4 %all-gather.2.cloned.1.call-start = ((), (), s32[]{:S(2)}) async-start(), calls=%async_computation.1 | async-start | bytes 1179648 | tf_op jit(solution)/shard_map/all_gather | solution.py:36
  7.9 71.0 %reduce-scatter.2.cloned.1.call-start = ((), (), s32[]{:S(2)}) async-start(), calls=%async_computation.2 | async-start | bytes 163840 | tf_op jit(solution)/shard_map/reduce_scatter | solution.py:51
  36.2 0.9 copy-start
  59.7 0.6 copy-start.2
  133.9 5.6 %copy-start.1 = (f32[128,64]{0,1:T(8,128)S(1)}, f32[128,64]{0,1:T(8,128)}, u32[]{:S(2)}) copy-start(f32[128,64]{0,1:T(8,128)} %reduce-scatter.2.cloned.1.call-done) | copy-start | bytes 98308
Sparse Core Ops, SparseCore 0:
  10.1 43.4 all-gather.1
  60.5 18.3 reduce-scatter.1
